TPU v7x, 32 devices: a whole 2x2x4 slice. The times are simulated.
32 devices in a mesh: dp: 8 (over z, x), seq: 4 (over y, core).
Axes of the slice: x: 2, y: 2, z: 4, core: 2. Of those that a mesh axis runs over, the one named last changes fastest.
Arguments:
- embeds: bfloat16 [16, 736, 1152], P('dp', 'seq'), may hold values from -6 to 6
- image_counts: int32 [8], P('dp'), may hold values from 1 to 2, as said below
- norm1_gain: float32 [1152], P('seq'), may hold values from 0.5 to 1.5
- norm1_bias: float32 [1152], P('seq'), may hold values from -3 to 3
- query_weight: float32 [1152, 1152], P('dp', 'seq'), may hold values from -0.1875 to 0.1875
- query_bias: float32 [1152], P('seq'), may hold values from -3 to 3
- key_weight: float32 [1152, 1152], P('dp', 'seq'), may hold values from -0.1875 to 0.1875
- value_weight: float32 [1152, 1152], P('dp', 'seq'), may hold values from -0.1875 to 0.1875
- value_bias: float32 [1152], P('seq'), may hold values from -3 to 3
- out_weight: float32 [1152, 1152], P('dp', 'seq'), may hold values from -1.5 to 1.5
- out_bias: float32 [1152], P('seq'), may hold values from -3 to 3
- norm2_gain: float32 [1152], P('seq'), may hold values from 0.5 to 1.5
- norm2_bias: float32 [1152], P('seq'), may hold values from -3 to 3
- fc1_weight: float32 [1152, 4304], P('dp', 'seq'), may hold values from -0.1875 to 0.1875
- fc1_bias: float32 [4304], P('seq'), may hold values from -3 to 3
- fc2_weight: float32 [1152, 4304], P('dp', 'seq'), may hold values from -0.09375 to 0.09375
- fc2_bias: float32 [1152], P('seq'), may hold values from -3 to 3
- out_grad: bfloat16 [16, 736, 1152], P('dp', 'seq'), may hold values from -6 to 6
Outputs:
- output: bfloat16 [16, 736, 1152], P('dp', 'seq')
- embeds_grad: bfloat16 [16, 736, 1152], P('dp', 'seq')
- norm1_gain_grad: float32 [1152], P('seq')
- norm1_bias_grad: float32 [1152], P('seq')
- query_weight_grad: float32 [1152, 1152], P('dp', 'seq')
- query_bias_grad: float32 [1152], P('seq')
- key_weight_grad: float32 [1152, 1152], P('dp', 'seq')
- value_weight_grad: float32 [1152, 1152], P('dp', 'seq')
- value_bias_grad: float32 [1152], P('seq')
- out_weight_grad: float32 [1152, 1152], P('dp', 'seq')
- out_bias_grad: float32 [1152], P('seq')
- norm2_gain_grad: float32 [1152], P('seq')
- norm2_bias_grad: float32 [1152], P('seq')
- fc1_weight_grad: float32 [1152, 4304], P('dp', 'seq')
- fc1_bias_grad: float32 [4304], P('seq')
- fc2_weight_grad: float32 [1152, 4304], P('dp', 'seq')
- fc2_bias_grad: float32 [1152], P('seq')
Inputs may be any that keep to these rules, and one draw needn't show every extreme that they name: The first image_counts[g] of group g's 2 image slots hold images, the others are empty; some group holds 2.
All inputs are finite; a program needn't handle non-finite values.
Results may differ from a plain program's by a relative error of at most 0.017.
Values may be sent and summed in bfloat16 or wider, within the bound.
A program may use at most 192 MiB of HBM per device.

v0:
```python
import jax
import jax.numpy as jnp
from jax import lax
from jax.sharding import PartitionSpec as P

HEAD_DIM = 72
SLOTS = 736
VALID = 729


EPSILON = 1e-06
NEGATIVE = -1000000000.0


def layer_norm(values, gain, shift):
    centred = values - jnp.mean(values, axis=-1, keepdims=True)
    spread = jnp.mean(centred * centred, axis=-1, keepdims=True)
    return centred * lax.rsqrt(spread + EPSILON) * gain + shift


def gelu_tanh(values):
    return jax.nn.gelu(values, approximate=True)


def times_weight(left_side, right_side):
    return jnp.dot(left_side, right_side, preferred_element_type=jnp.float32)


def times_transposed(left_side, right_side):
    return lax.dot_general(
        left_side, right_side, (((1,), (1,)), ((), ())), preferred_element_type=jnp.float32
    )


def outer_sum(left_side, right_side):
    return lax.dot_general(
        left_side, right_side, (((0,), (0,)), ((), ())), preferred_element_type=jnp.float32
    )


def split_heads(stacked):
    slot_count = stacked.shape[1]
    local_heads = stacked.shape[2] // HEAD_DIM
    return (
        stacked[0].reshape(slot_count, local_heads, HEAD_DIM),
        stacked[1].reshape(slot_count, local_heads, HEAD_DIM),
        stacked[2].reshape(slot_count, local_heads, HEAD_DIM),
    )


def head_scores(query_heads, key_heads, slot_live):
    scores = jnp.einsum(
        "qhd,khd->hqk", query_heads, key_heads, preferred_element_type=jnp.float32
    ) * HEAD_DIM ** (-0.5)
    return jnp.where(slot_live[None, None, :], scores, NEGATIVE)


def attend_image(stacked, slot_live):
    query_heads, key_heads, value_heads = split_heads(stacked)
    scores = head_scores(query_heads, key_heads, slot_live)
    highest = jnp.max(scores, axis=-1, keepdims=True)
    raised = jnp.exp(scores - highest)
    total = jnp.sum(raised, axis=-1, keepdims=True)
    probs = (raised / total).astype(jnp.bfloat16)
    context = jnp.einsum("hqk,khd->qhd", probs, value_heads, preferred_element_type=jnp.float32)
    context = context.reshape(stacked.shape[1], stacked.shape[2]).astype(jnp.bfloat16)
    return (context, (highest + jnp.log(total))[..., 0])


def attend_back(stacked, log_total, grad_context, slot_live):
    query_heads, key_heads, value_heads = split_heads(stacked)
    grad_heads = grad_context.reshape(query_heads.shape)
    scores = head_scores(query_heads, key_heads, slot_live)
    probs = jnp.exp(scores - log_total[..., None])
    grad_probs = jnp.einsum(
        "qhd,khd->hqk", grad_heads, value_heads, preferred_element_type=jnp.float32
    )
    row_inner = jnp.sum(probs * grad_probs, axis=-1, keepdims=True)
    grad_scores = (probs * (grad_probs - row_inner)).astype(jnp.bfloat16)
    scale = HEAD_DIM ** (-0.5)
    grad_query = (
        jnp.einsum("hqk,khd->qhd", grad_scores, key_heads, preferred_element_type=jnp.float32)
        * scale
    )
    grad_key = (
        jnp.einsum("hqk,qhd->khd", grad_scores, query_heads, preferred_element_type=jnp.float32)
        * scale
    )
    grad_value = jnp.einsum(
        "hqk,qhd->khd", probs.astype(jnp.bfloat16), grad_heads, preferred_element_type=jnp.float32
    )
    shape_out = (stacked.shape[1], stacked.shape[2])
    return jnp.stack(
        [
            grad_query.reshape(shape_out).astype(jnp.bfloat16),
            grad_key.reshape(shape_out).astype(jnp.bfloat16),
            grad_value.reshape(shape_out).astype(jnp.bfloat16),
        ],
        axis=0,
    )


def per_device(
    embeds,
    image_counts,
    norm1_gain,
    norm1_bias,
    query_weight,
    query_bias,
    key_weight,
    value_weight,
    value_bias,
    out_weight,
    out_bias,
    norm2_gain,
    norm2_bias,
    fc1_weight,
    fc1_bias,
    fc2_weight,
    fc2_bias,
    out_grad,
):
    images, rows_dev, width = embeds.shape
    token_count = images * rows_dev
    position = lax.axis_index("seq") * rows_dev + jnp.arange(rows_dev, dtype=jnp.int32)
    slot_live = jnp.arange(SLOTS, dtype=jnp.int32) < VALID
    image_live = jnp.arange(images, dtype=jnp.int32) < image_counts[0]
    row_mask = (
        jnp.where(image_live[:, None] & (position < VALID)[None, :], 1.0, 0.0)
        .astype(jnp.float32)
        .reshape(token_count)
    )
    query_low = query_weight.astype(jnp.bfloat16)
    key_low = key_weight.astype(jnp.bfloat16)
    value_low = value_weight.astype(jnp.bfloat16)
    attend_low = out_weight.astype(jnp.bfloat16)
    first_low = fc1_weight.astype(jnp.bfloat16)
    second_low = fc2_weight.astype(jnp.bfloat16)
    gathered = (
        lax.all_gather(query_low, "seq", axis=1, tiled=True),
        lax.all_gather(key_low, "seq", axis=1, tiled=True),
        lax.all_gather(value_low, "seq", axis=1, tiled=True),
        lax.all_gather(attend_low, "seq", axis=1, tiled=True),
        lax.all_gather(first_low, "seq", axis=1, tiled=True),
        lax.all_gather(second_low, "seq", axis=1, tiled=True),
        lax.all_gather(norm1_gain.astype(jnp.bfloat16), "seq", axis=0, tiled=True),
        lax.all_gather(norm1_bias.astype(jnp.bfloat16), "seq", axis=0, tiled=True),
        lax.all_gather(query_bias.astype(jnp.bfloat16), "seq", axis=0, tiled=True),
        lax.all_gather(value_bias.astype(jnp.bfloat16), "seq", axis=0, tiled=True),
        lax.all_gather(out_bias.astype(jnp.bfloat16), "seq", axis=0, tiled=True),
        lax.all_gather(norm2_gain.astype(jnp.bfloat16), "seq", axis=0, tiled=True),
        lax.all_gather(norm2_bias.astype(jnp.bfloat16), "seq", axis=0, tiled=True),
        lax.all_gather(fc2_bias.astype(jnp.bfloat16), "seq", axis=0, tiled=True),
        lax.all_gather(fc1_bias.astype(jnp.bfloat16), "seq", axis=0, tiled=True),
    )
    query_part, key_part, value_part, attend_part, first_part, second_part = gathered[:6]
    vectors = [element.astype(jnp.float32) for element in gathered[6:]]
    (
        gain_one,
        bias_one,
        query_shift,
        value_shift,
        attend_shift,
        gain_two,
        bias_two,
        second_shift,
        first_shift,
    ) = vectors
    query_full, key_full, value_full, attend_full, first_full, second_full = (
        lax.all_gather(query_part, "dp", axis=0, tiled=True),
        lax.all_gather(key_part, "dp", axis=0, tiled=True),
        lax.all_gather(value_part, "dp", axis=0, tiled=True),
        lax.all_gather(attend_part, "dp", axis=0, tiled=True),
        lax.all_gather(first_part, "dp", axis=0, tiled=True),
        lax.all_gather(second_part, "dp", axis=0, tiled=True),
    )
    embed_rows = embeds.reshape(token_count, width).astype(jnp.float32)
    normed_one = layer_norm(embed_rows, gain_one, bias_one).astype(jnp.bfloat16)
    queries = (times_weight(normed_one, query_full) + query_shift).astype(jnp.bfloat16)
    key_rows = times_weight(normed_one, key_full).astype(jnp.bfloat16)
    value_rows = (times_weight(normed_one, value_full) + value_shift).astype(jnp.bfloat16)
    stacked = jnp.stack(
        [
            queries.reshape(images, rows_dev, width),
            key_rows.reshape(images, rows_dev, width),
            value_rows.reshape(images, rows_dev, width),
        ],
        axis=1,
    )
    by_heads = lax.all_to_all(stacked, "seq", split_axis=3, concat_axis=2, tiled=True)
    context_heads, log_total = lax.map(lambda element: attend_image(element, slot_live), by_heads)
    context = lax.all_to_all(context_heads, "seq", split_axis=1, concat_axis=2, tiled=True).reshape(
        token_count, width
    )
    residual = embed_rows + times_weight(context, attend_full) + attend_shift
    normed_two = layer_norm(residual, gain_two, bias_two).astype(jnp.bfloat16)
    inner = times_weight(normed_two, first_full) + first_shift
    activated = gelu_tanh(inner).astype(jnp.bfloat16)
    mixed = times_transposed(activated, second_full) + second_shift
    output = (
        ((residual + mixed) * row_mask[:, None])
        .astype(jnp.bfloat16)
        .reshape(images, rows_dev, width)
    )
    query_again, key_again, value_again, attend_again, first_again, second_again = (
        lax.all_gather(query_low, "seq", axis=1, tiled=True),
        lax.all_gather(key_low, "seq", axis=1, tiled=True),
        lax.all_gather(value_low, "seq", axis=1, tiled=True),
        lax.all_gather(attend_low, "seq", axis=1, tiled=True),
        lax.all_gather(first_low, "seq", axis=1, tiled=True),
        lax.all_gather(second_low, "seq", axis=1, tiled=True),
    )
    query_back, key_back, value_back, attend_back_mat, first_back, second_back = (
        lax.all_gather(query_again, "dp", axis=0, tiled=True),
        lax.all_gather(key_again, "dp", axis=0, tiled=True),
        lax.all_gather(value_again, "dp", axis=0, tiled=True),
        lax.all_gather(attend_again, "dp", axis=0, tiled=True),
        lax.all_gather(first_again, "dp", axis=0, tiled=True),
        lax.all_gather(second_again, "dp", axis=0, tiled=True),
    )
    grad_mixed = out_grad.reshape(token_count, width).astype(jnp.float32) * row_mask[:, None]
    grad_mixed_low = grad_mixed.astype(jnp.bfloat16)
    second_shift_grad = jnp.sum(grad_mixed, axis=0)
    grad_active = times_weight(grad_mixed_low, second_back)
    gelu_pull = jax.vjp(gelu_tanh, inner)[1]
    grad_inner = gelu_pull(grad_active)[0].astype(jnp.bfloat16)
    grad_normed_two = times_transposed(grad_inner, first_back)
    norm_two_pull = jax.vjp(layer_norm, residual, gain_two, bias_two)[1]
    grad_norm_input, gain_two_grad, bias_two_grad = norm_two_pull(grad_normed_two)
    grad_residual = grad_mixed + grad_norm_input
    grad_attended = grad_residual.astype(jnp.bfloat16)
    grad_context = times_transposed(grad_attended, attend_back_mat).astype(jnp.bfloat16)
    grad_heads = lax.all_to_all(
        grad_context.reshape(images, rows_dev, width),
        "seq",
        split_axis=2,
        concat_axis=1,
        tiled=True,
    )
    grad_stacked = lax.map(
        lambda element: attend_back(element[0], element[1], element[2], slot_live),
        (by_heads, log_total, grad_heads),
    )
    returned = lax.all_to_all(grad_stacked, "seq", split_axis=2, concat_axis=3, tiled=True)
    grad_queries = returned[:, 0].reshape(token_count, width)
    grad_keys = returned[:, 1].reshape(token_count, width)
    grad_values = returned[:, 2].reshape(token_count, width)
    grad_normed_one = (
        times_transposed(grad_queries, query_back)
        + times_transposed(grad_keys, key_back)
        + times_transposed(grad_values, value_back)
    )
    norm_one_pull = jax.vjp(layer_norm, embed_rows, gain_one, bias_one)[1]
    grad_embed_norm, gain_one_grad, bias_one_grad = norm_one_pull(grad_normed_one)
    embeds_grad = (
        (grad_residual + grad_embed_norm).astype(jnp.bfloat16).reshape(images, rows_dev, width)
    )
    query_cols, key_cols, value_cols, attend_cols, inner_cols, active_cols = (
        lax.all_to_all(grad_queries, "seq", split_axis=1, concat_axis=0, tiled=True),
        lax.all_to_all(grad_keys, "seq", split_axis=1, concat_axis=0, tiled=True),
        lax.all_to_all(grad_values, "seq", split_axis=1, concat_axis=0, tiled=True),
        lax.all_to_all(grad_attended, "seq", split_axis=1, concat_axis=0, tiled=True),
        lax.all_to_all(grad_inner, "seq", split_axis=1, concat_axis=0, tiled=True),
        lax.all_to_all(activated, "seq", split_axis=1, concat_axis=0, tiled=True),
    )
    one_piece = lax.all_gather(normed_one, "seq", axis=0, tiled=True)
    context_piece = lax.all_gather(context, "seq", axis=0, tiled=True)
    two_piece = lax.all_gather(normed_two, "seq", axis=0, tiled=True)
    mixed_piece = lax.all_gather(grad_mixed_low, "seq", axis=0, tiled=True)
    matrices = (
        lax.psum_scatter(
            outer_sum(one_piece, query_cols).astype(jnp.bfloat16),
            "dp",
            scatter_dimension=0,
            tiled=True,
        ).astype(jnp.float32),
        lax.psum_scatter(
            outer_sum(one_piece, key_cols).astype(jnp.bfloat16),
            "dp",
            scatter_dimension=0,
            tiled=True,
        ).astype(jnp.float32),
        lax.psum_scatter(
            outer_sum(one_piece, value_cols).astype(jnp.bfloat16),
            "dp",
            scatter_dimension=0,
            tiled=True,
        ).astype(jnp.float32),
        lax.psum_scatter(
            outer_sum(context_piece, attend_cols).astype(jnp.bfloat16),
            "dp",
            scatter_dimension=0,
            tiled=True,
        ).astype(jnp.float32),
        lax.psum_scatter(
            outer_sum(two_piece, inner_cols).astype(jnp.bfloat16),
            "dp",
            scatter_dimension=0,
            tiled=True,
        ).astype(jnp.float32),
        lax.psum_scatter(
            outer_sum(mixed_piece, active_cols).astype(jnp.bfloat16),
            "dp",
            scatter_dimension=0,
            tiled=True,
        ).astype(jnp.float32),
    )
    owned = (
        lax.psum_scatter(gain_one_grad, "seq", scatter_dimension=0, tiled=True),
        lax.psum_scatter(bias_one_grad, "seq", scatter_dimension=0, tiled=True),
        lax.psum_scatter(gain_two_grad, "seq", scatter_dimension=0, tiled=True),
        lax.psum_scatter(bias_two_grad, "seq", scatter_dimension=0, tiled=True),
        lax.psum_scatter(second_shift_grad, "seq", scatter_dimension=0, tiled=True),
    )
    query_shift_grad = jnp.sum(query_cols.astype(jnp.float32), axis=0)
    value_shift_grad = jnp.sum(value_cols.astype(jnp.float32), axis=0)
    attend_shift_grad = jnp.sum(attend_cols.astype(jnp.float32), axis=0)
    first_shift_grad = jnp.sum(inner_cols.astype(jnp.float32), axis=0)
    vector_sums = lax.psum(
        (
            owned[0],
            owned[1],
            query_shift_grad,
            value_shift_grad,
            attend_shift_grad,
            owned[2],
            owned[3],
            owned[4],
            first_shift_grad,
        ),
        "dp",
    )
    return (
        output,
        embeds_grad,
        vector_sums[0],
        vector_sums[1],
        matrices[0],
        vector_sums[2],
        matrices[1],
        matrices[2],
        vector_sums[3],
        matrices[3],
        vector_sums[4],
        vector_sums[5],
        vector_sums[6],
        matrices[4],
        vector_sums[8],
        matrices[5],
        vector_sums[7],
    )


def solution(mesh):
    in_specs = (
        P("dp", "seq", None),
        P("dp"),
        P("seq"),
        P("seq"),
        P("dp", "seq"),
        P("seq"),
        P("dp", "seq"),
        P("dp", "seq"),
        P("seq"),
        P("dp", "seq"),
        P("seq"),
        P("seq"),
        P("seq"),
        P("dp", "seq"),
        P("seq"),
        P("dp", "seq"),
        P("seq"),
        P("dp", "seq", None),
    )
    out_specs = (
        P("dp", "seq", None),
        P("dp", "seq", None),
        P("seq"),
        P("seq"),
        P("dp", "seq"),
        P("seq"),
        P("dp", "seq"),
        P("dp", "seq"),
        P("seq"),
        P("dp", "seq"),
        P("seq"),
        P("seq"),
        P("seq"),
        P("dp", "seq"),
        P("seq"),
        P("dp", "seq"),
        P("seq"),
    )
    return jax.shard_map(
        per_device, mesh=mesh, in_specs=in_specs, out_specs=out_specs, check_vma=False
    )
```

profile of v0, /device:TPU:0, one launch (start us, length us, event | category | flops | bytes accessed | tf_op | source)
XLA Modules:
  0.0 1177.7 jit_solution(9780599162972016104)
XLA Ops:
  11.3 8.4 all-gather.2
  20.9 9.8 all-gather.1
  40.2 8.2 all-gather.3
  63.0 12.5 %all-reduce.16 = (bf16[1152]{0:T(1024)(128)(2,1)S(1)}, bf16[1152]{0:T(1024)(128)(2,1)S(1)}, bf16[1152]{0:T(1024)(128)(2,1)S(1)}, bf16[1152]{0:T(1024)(128)(2,1)S...) all-reduce(bf16[1152]{0:T(1024)(128)(2,1)S(1)} %dynamic-update-slic, ...), channel_id=1, replica_groups=mesh['dp'=8,'seq'=4] {'seq'}, use_global_device_ids=true, to_apply=%add.1 | all-reduce | flops 13520 | bytes 54080
  77.6 35.8 %all-gather.23.cloned.1.call-done = bf16[1152,1152]{1,0:T(8,128)(2,1)} async-done(((bf16[144,1152]{1,0:T(8,128)(2,1)}), bf16[1152,1152]{1,0:T(8,128)(2,1)}) %all-gather.23.cloned.1.call-update) | async-done | bytes 2654224 | tf_op jit(solution)/shard_map/all_gather | solution.py:172
  121.0 48.6 %all-gather.21.cloned.1.call-done = bf16[1152,1152]{1,0:T(8,128)(2,1)} async-done(((bf16[144,1152]{1,0:T(8,128)(2,1)}), bf16[1152,1152]{1,0:T(8,128)(2,1)}) %all-gather.21.cloned.1.call-update) | async-done | bytes 2654224 | tf_op jit(solution)/shard_map/all_gather | solution.py:171
  177.1 48.0 %all-gather.19.cloned.1.call-done = bf16[1152,1152]{1,0:T(8,128)(2,1)} async-done(((bf16[144,1152]{1,0:T(8,128)(2,1)}), bf16[1152,1152]{1,0:T(8,128)(2,1)}) %all-gather.19.cloned.1.call-update) | async-done | bytes 2654224 | tf_op jit(solution)/shard_map/all_gather | solution.py:170
  233.5 8.2 pad_maximum_fusion
  246.7 40.9 %all-to-all-done = bf16[2,3,184,1152]{2,0,1,3:T(2,128)(2,1)} async-done(((bf16[2,3,184,1152]{2,0,1,3:T(2,128)(2,1)}), bf16[2,3,184,1152]{2,0,1,3:T(2,128)(2,1)}, u32[]{:S(2)}, u32[]{:S(2)}) %all-to-all-start) | async-done | bytes 2543648 | tf_op jit(solution)/shard_map/all_to_all | solution.py:190
  287.6 7.1 copy.178
  300.8 15.8 %while.24 = (s32[]{:T(128)}, bf16[2,736,288]{1,2,0:T(8,128)(2,1)}, f32[2,4,736]{2,1,0:T(4,128)S(1)}, bf16[2,3,736,288]{2,3,1,0:T(8,128)(2,1)S(1)}, s32[]{:T(128)}, /*index=5*/s32[]{:T(128)}, s32[]{}, s32[]{}) while((s32[]{:T(128)}, bf16[2,736,288]{1,2,0:T(8,128)(2,1)}, f32[2,4,736]{2,1,0:T(4,128)S(1)}, ...), condition=%wide.region_5.6_spmd.clone, body=%wide.region_2.5_spmd.clone.sunk | while | flops 650244992 | bytes 38007360 | solution.py:191
  321.2 18.8 %all_to_all.183 = bf16[2,736,288]{2,0,1:T(2,128)(2,1)S(1)} all-to-all(bf16[2,736,288]{2,0,1:T(2,128)(2,1)} %copy.136), channel_id=1, replica_groups=mesh['dp'=8,'seq'=4] {'seq'}, dimensions={1} | all-to-all | bytes 1695744 | tf_op jit(solution)/shard_map/all_to_all | solution.py:192
  355.8 70.6 %all-gather.29.cloned.1.call-done = bf16[1152,4304]{1,0:T(8,128)(2,1)} async-done(((bf16[144,4304]{1,0:T(8,128)(2,1)}), bf16[1152,4304]{1,0:T(8,128)(2,1)}) %all-gather.29.cloned.1.call-update) | async-done | bytes 9916432 | tf_op jit(solution)/shard_map/all_gather | solution.py:175
  426.3 11.2 fusion.44
  437.5 134.0 %all-gather.27.cloned.1.call-done = bf16[1152,4304]{1,0:T(8,128)(2,1)} async-done(((bf16[144,4304]{1,0:T(8,128)(2,1)}), bf16[1152,4304]{1,0:T(8,128)(2,1)}) %all-gather.27.cloned.1.call-update) | async-done | bytes 9916432 | tf_op jit(solution)/shard_map/all_gather | solution.py:174
  571.6 13.4 %fusion.28 = (bf16[368,4304]{1,0:T(8,128)(2,1)S(1)}, bf16[368,4304]{1,0:T(8,128)(2,1)}) fusion(f32[368,4304]{1,0:T(8,128)} %fusion.44, f32[4304]{0:T(1024)} %convert_element_type.280, bf16[368,1152]{1,0:T(8,128)(2,1)S(1)} %copy-done.15, bf16[1152,4304]{1,0:T(8,128)(2,1)} %all-gather.27.cloned.1.call-done), kind=kOutput, calls=%fused_computation.50 | convolution fusion | flops 3685670144 | bytes 23452480 | tf_op jit(solution)/shard_map/dot_general | solution.py:26
  586.7 9.1 multiply_reduce_fusion.2
  611.4 25.8 %all-to-all-done.2 = bf16[2,184,1152]{1,0,2:T(2,128)(2,1)} async-done(((bf16[2,184,1152]{1,0,2:T(2,128)(2,1)}), bf16[2,184,1152]{1,0,2:T(2,128)(2,1)}, u32[]{:S(2)}, u32[]{:S(2)}) %all-to-all-start.2) | async-done | bytes 847904 | tf_op jit(solution)/shard_map/all_to_all | solution.py:233
  648.1 31.3 %while.25 = (s32[]{:T(128)}, bf16[2,3,736,288]{2,3,1,0:T(8,128)(2,1)}, bf16[2,3,736,288]{2,3,1,0:T(8,128)(2,1)S(1)}, f32[2,4,736]{2,1,0:T(4,128)S(1)}, bf16[2,73...) while((s32[]{:T(128)}, bf16[2,3,736,288]{2,3,1,0:T(8,128)(2,1)}, ...), condition=%wide.region_12.13_spmd.clone, body=%wide.region_10.12_spmd.clone.sunk | while | flops 1597459328 | bytes 95723080 | solution.py:240
  679.4 12.0 %copy.145 = bf16[2,3,736,288]{3,0,1,2:T(2,128)(2,1)} copy(bf16[2,3,736,288]{2,3,1,0:T(8,128)(2,1)} %get-tuple-element.79) | data formatting | bytes 5087232 | tf_op jit(solution)/shard_map/while | solution.py:240
  700.6 40.5 %all-to-all-done.3 = bf16[2,3,736,288]{3,0,1,2:T(2,128)(2,1)S(1)} async-done(((bf16[2,3,736,288]{3,0,1,2:T(2,128)(2,1)}), bf16[2,3,736,288]{3,0,1,2:T(2,128)(2,1)S(1)}, u32[]{:S(2)}, u32[]{:S(2)}) %all-to-all-start.3) | async-done | bytes 2543648 | tf_op jit(solution)/shard_map/all_to_all | solution.py:244
  834.7 17.7 %all-to-all-done.8 = bf16[368,4,1076]{0,2,1:T(8,128)(2,1)S(1)} async-done(((bf16[368,4,1076]{0,2,1:T(8,128)(2,1)}), bf16[368,4,1076]{0,2,1:T(8,128)(2,1)S(1)}, u32[]{:S(2)}, u32[]{:S(2)}) %all-to-all-start.8) | async-done | bytes 3167776 | tf_op jit(solution)/shard_map/all_to_all | solution.py:263
  856.3 9.4 convolution_convert_fusion.1
  865.7 7.9 reshape.351
  873.6 7.4 copy.173
  888.1 36.7 %all-to-all-done.9 = bf16[368,4,1076]{0,2,1:T(8,128)(2,1)} async-done(((bf16[368,4,1076]{0,2,1:T(8,128)(2,1)}), bf16[368,4,1076]{0,2,1:T(8,128)(2,1)}, u32[]{:S(2)}, u32[]{:S(2)}) %all-to-all-start.9) | async-done | bytes 3167776 | tf_op jit(solution)/shard_map/all_to_all | solution.py:264
  930.5 9.3 convolution_convert_fusion
  940.5 10.6 fusion.32
  963.0 10.5 all-reduce.15
  982.3 38.0 %all-reduce.14 = (f32[288]{0:T(512)}, f32[288]{0:T(512)}, f32[288]{0:T(512)}, f32[288]{0:T(512)}, f32[288]{0:T(512)}, /*index=5*/f32[288]{0:T(512)}, f32[288]{0:T(512)}, f32[1076]{0:T(1024)}, f32[288]{0:T(512)}) all-reduce(f32[288]{0:T(512)S(1)} %dynamic-slice.10, ...), channel_id=1, replica_groups=mesh['dp'=8,'seq'=4] {'dp'}, use_global_device_ids=true, to_apply=%region_17.18 | all-reduce | flops 3380 | bytes 27040 | tf_op jit(solution)/shard_map/psum | solution.py:319
  1025.1 69.4 %reduce-scatter.15.cloned.1.call-done = bf16[144,1076]{1,0:T(8,128)(2,1)} async-done(((bf16[1152,1076]{1,0:T(8,128)(2,1)}), bf16[144,1076]{1,0:T(8,128)(2,1)}) %reduce-scatter.15.cloned.1.call-update) | async-done | bytes 309904 | tf_op jit(solution)/shard_map/reduce_scatter | solution.py:295
  1096.4 72.3 %reduce-scatter.17.cloned.1.call-done = bf16[144,1076]{1,0:T(8,128)(2,1)} async-done(((bf16[1152,1076]{1,0:T(8,128)(2,1)}), bf16[144,1076]{1,0:T(8,128)(2,1)}) %reduce-scatter.17.cloned.1.call-update) | async-done | bytes 309904 | tf_op jit(solution)/shard_map/reduce_scatter | solution.py:301
  (373 shorter events, 307.2 us)
Async XLA Ops:
  7.2 42.5 %all-gather.41.cloned.1.call-start = ((), (), s32[]{:S(2)}) async-start(), calls=%async_computation.33 | async-start | bytes 1658880 | tf_op jit(solution)/shard_map/all_gather | solution.py:145
  9.2 45.6 %all-gather.39.cloned.1.call-start = ((), (), s32[]{:S(2)}) async-start(), calls=%async_computation.32 | async-start | bytes 1658880 | tf_op jit(solution)/shard_map/all_gather | solution.py:144
  11.2 102.2 %all-gather.23.cloned.1.call-start = ((), (), s32[]{:S(2)}) async-start(), calls=%async_computation.18 | async-start | bytes 2985984 | tf_op jit(solution)/shard_map/all_gather | solution.py:172
  20.8 148.7 %all-gather.21.cloned.1.call-start = ((), (), s32[]{:S(2)}) async-start(), calls=%async_computation.17 | async-start | bytes 2985984 | tf_op jit(solution)/shard_map/all_gather | solution.py:171
  32.0 193.2 %all-gather.19.cloned.1.call-start = ((), (), s32[]{:S(2)}) async-start(), calls=%async_computation.16 | async-start | bytes 2985984 | tf_op jit(solution)/shard_map/all_gather | solution.py:170
  40.1 309.7 %all-gather.25.cloned.1.call-start = ((), (), s32[]{:S(2)}) async-start(), calls=%async_computation.19 | async-start | bytes 2985984 | tf_op jit(solution)/shard_map/all_gather | solution.py:173
  49.7 376.7 %all-gather.29.cloned.1.call-start = ((), (), s32[]{:S(2)}) async-start(), calls=%async_computation.21 | async-start | bytes 11280384 | tf_op jit(solution)/shard_map/all_gather | solution.py:175
  53.6 518.0 %all-gather.27.cloned.1.call-start = ((), (), s32[]{:S(2)}) async-start(), calls=%async_computation.20 | async-start | bytes 11280384 | tf_op jit(solution)/shard_map/all_gather | solution.py:174
  60.9 56.5 %copy-start.34 = (f32[368]{0:T(512)}, f32[368]{0:T(512)S(1)}, u32[]{:S(2)}) copy-start(f32[368]{0:T(512)S(1)} %div.51) | copy-start | bytes 4420
  75.5 41.9 %copy-start.30 = (f32[1152]{0:T(1024)}, f32[1152]{0:T(1024)S(1)}, u32[]{:S(2)}) copy-start(f32[1152]{0:T(1024)S(1)} %convert_element_type.256) | copy-start | bytes 13828
  77.6 92.0 %copy-start.18 = (bf16[368,1152]{1,0:T(8,128)(2,1)}, bf16[368,1152]{1,0:T(8,128)(2,1)S(1)}, u32[]{:S(2)}) copy-start(bf16[368,1152]{1,0:T(8,128)(2,1)S(1)} %get-tuple-element.167) | copy-start | bytes 2543620
  241.7 45.9 %all-to-all-start = ((bf16[2,3,184,1152]{2,0,1,3:T(2,128)(2,1)}), bf16[2,3,184,1152]{2,0,1,3:T(2,128)(2,1)}, u32[]{:S(2)}, u32[]{:S(2)}) async-start(bf16[2,3,184,1152]{2,0,1,3:T(2,128)(2,1)} %pad_maximum_fusion), calls=%async_computation | async-start | bytes 7077888 | tf_op jit(solution)/shard_map/all_to_all | solution.py:190
  246.5 512.8 %all-gather.33.cloned.1.call-start = ((), (), s32[]{:S(2)}) async-start(), calls=%async_computation.26 | async-start | bytes 4239360 | tf_op jit(solution)/shard_map/all_gather | solution.py:267
  344.3 448.4 %all-gather.31.cloned.1.call-start = ((), (), s32[]{:S(2)}) async-start(), calls=%async_computation.22 | async-start | bytes 4239360 | tf_op jit(solution)/shard_map/all_gather | solution.py:266
  344.9 511.4 %all-gather.35.cloned.1.call-start = ((), (), s32[]{:S(2)}) async-start(), calls=%async_computation.28 | async-start | bytes 4239360 | tf_op jit(solution)/shard_map/all_gather | solution.py:268
  346.9 249.5 %copy-start.32 = (f32[368]{0:T(512)}, f32[368]{0:T(512)S(1)}, u32[]{:S(2)}) copy-start(f32[368]{0:T(512)S(1)} %select_n.20) | copy-start | bytes 4420
  355.7 215.8 %copy-start.15 = (bf16[368,1152]{1,0:T(8,128)(2,1)S(1)}, bf16[368,1152]{1,0:T(8,128)(2,1)}, u32[]{:S(2)}) copy-start(bf16[368,1152]{1,0:T(8,128)(2,1)} %add_convert_fusion.1) | copy-start | bytes 2543620
  605.2 32.0 %all-to-all-start.2 = ((bf16[2,184,1152]{1,0,2:T(2,128)(2,1)}), bf16[2,184,1152]{1,0,2:T(2,128)(2,1)}, u32[]{:S(2)}, u32[]{:S(2)}) async-start(bf16[2,184,1152]{1,0,2:T(2,128)(2,1)} %copy.142), calls=%async_computation.2 | async-start | bytes 2359296 | tf_op jit(solution)/shard_map/all_to_all | solution.py:233
  609.5 321.0 %all-gather.37.cloned.1.call-start = ((), (), s32[]{:S(2)}) async-start(), calls=%async_computation.30 | async-start | bytes 4239360 | tf_op jit(solution)/shard_map/all_gather | solution.py:269
  637.2 54.2 %all-to-all-start.7 = ((bf16[368,4,288]{0,2,1:T(8,128)(2,1)}), bf16[368,4,288]{0,2,1:T(8,128)(2,1)}, u32[]{:S(2)}, u32[]{:S(2)}) async-start(bf16[368,4,288]{0,2,1:T(8,128)(2,1)} %bitcast.47), calls=%async_computation.10 | async-start | bytes 1769472 | tf_op jit(solution)/shard_map/all_to_all | solution.py:262
  691.5 49.7 %all-to-all-start.3 = ((bf16[2,3,736,288]{3,0,1,2:T(2,128)(2,1)}), bf16[2,3,736,288]{3,0,1,2:T(2,128)(2,1)S(1)}, u32[]{:S(2)}, u32[]{:S(2)}) async-start(bf16[2,3,736,288]{3,0,1,2:T(2,128)(2,1)} %copy.145), calls=%async_computation.3 | async-start | bytes 6782976 | tf_op jit(solution)/shard_map/all_to_all | solution.py:244
  755.7 16.2 %all-to-all-start.4 = ((bf16[368,4,288]{0,2,1:T(8,128)(2,1)}), bf16[368,4,288]{0,2,1:T(8,128)(2,1)S(1)}, u32[]{:S(2)}, u32[]{:S(2)}) async-start(bf16[368,4,288]{0,2,1:T(8,128)(2,1)} %copy.148), calls=%async_computation.4 | async-start | bytes 1769472 | tf_op jit(solution)/shard_map/all_to_all | solution.py:259
  759.2 193.4 %reduce-scatter.13.cloned.1.call-start = ((), (), s32[]{:S(2)}) async-start(), calls=%async_computation.27 | async-start | bytes 995328 | tf_op jit(solution)/shard_map/reduce_scatter | solution.py:289
  771.8 16.2 %all-to-all-start.6 = ((bf16[368,4,288]{0,2,1:T(8,128)(2,1)}), bf16[368,4,288]{0,2,1:T(8,128)(2,1)S(1)}, u32[]{:S(2)}, u32[]{:S(2)}) async-start(bf16[368,4,288]{0,2,1:T(8,128)(2,1)} %copy.152), calls=%async_computation.8 | async-start | bytes 1769472 | tf_op jit(solution)/shard_map/all_to_all | solution.py:261
  788.0 21.9 %all-to-all-start.5 = ((bf16[368,4,288]{0,2,1:T(8,128)(2,1)}), bf16[368,4,288]{0,2,1:T(8,128)(2,1)}, u32[]{:S(2)}, u32[]{:S(2)}) async-start(bf16[368,4,288]{0,2,1:T(8,128)(2,1)} %copy.150), calls=%async_computation.6 | async-start | bytes 1769472 | tf_op jit(solution)/shard_map/all_to_all | solution.py:260
  792.6 227.7 %reduce-scatter.7.cloned.1.call-start = ((), (), s32[]{:S(2)}) async-start(), calls=%async_computation.23 | async-start | bytes 995328 | tf_op jit(solution)/shard_map/reduce_scatter | solution.py:271
  809.9 42.4 %all-to-all-start.8 = ((bf16[368,4,1076]{0,2,1:T(8,128)(2,1)}), bf16[368,4,1076]{0,2,1:T(8,128)(2,1)S(1)}, u32[]{:S(2)}, u32[]{:S(2)}) async-start(bf16[368,4,1076]{0,2,1:T(8,128)(2,1)} %copy.172), calls=%async_computation.12 | async-start | bytes 6635520 | tf_op jit(solution)/shard_map/all_to_all | solution.py:263
  813.6 208.3 %reduce-scatter.9.cloned.1.call-start = ((), (), s32[]{:S(2)}) async-start(), calls=%async_computation.24 | async-start | bytes 995328 | tf_op jit(solution)/shard_map/reduce_scatter | solution.py:277
  824.1 199.4 %reduce-scatter.11.cloned.1.call-start = ((), (), s32[]{:S(2)}) async-start(), calls=%async_computation.25 | async-start | bytes 995328 | tf_op jit(solution)/shard_map/reduce_scatter | solution.py:283
  834.5 260.1 %reduce-scatter.15.cloned.1.call-start = ((), (), s32[]{:S(2)}) async-start(), calls=%async_computation.29 | async-start | bytes 2985984 | tf_op jit(solution)/shard_map/reduce_scatter | solution.py:295
  881.1 43.7 %all-to-all-start.9 = ((bf16[368,4,1076]{0,2,1:T(8,128)(2,1)}), bf16[368,4,1076]{0,2,1:T(8,128)(2,1)}, u32[]{:S(2)}, u32[]{:S(2)}) async-start(bf16[368,4,1076]{0,2,1:T(8,128)(2,1)} %copy.173), calls=%async_computation.14 | async-start | bytes 6635520 | tf_op jit(solution)/shard_map/all_to_all | solution.py:264
  885.9 282.8 %reduce-scatter.17.cloned.1.call-start = ((), (), s32[]{:S(2)}) async-start(), calls=%async_computation.31 | async-start | bytes 2985984 | tf_op jit(solution)/shard_map/reduce_scatter | solution.py:301
  (61 other events, 374.1 us)
Sparse Core Ops, SparseCore 0:
  10.2 23.3 all-gather.40
  35.7 19.0 all-gather.38
  57.5 55.7 all-gather.22
  116.0 53.5 all-gather.20
  171.6 53.5 all-gather.18
  227.2 53.5 all-gather.24
  282.9 143.3 all-gather.28
  428.5 142.9 all-gather.26
  573.7 28.0 all-gather.32
  603.8 41.2 all-gather.30
  646.6 28.3 all-gather.34
  676.4 36.1 all-gather.36
  764.4 63.5 reduce-scatter.12
  831.2 60.9 reduce-scatter.6
  895.5 60.9 reduce-scatter.8
  959.7 60.9 reduce-scatter.10
  1024.2 70.2 reduce-scatter.14
  1098.0 70.6 reduce-scatter.16
where the time goes:
time: 1190 us; the launch traced here: 1180 us
  waiting for transfers between devices  654 us (55%)
  local copies, waits for them, and re-layouts  166 us (14%)
  matrix products  134 us (11%)
  blocking collectives  113 us (9%)
  other arithmetic  53 us (4%)
  starting transfers between devices  39.1 us (3%)
  between operations  18.3 us (2%)
    all_gather x1, waiting for transfers between devices, per_device(): lax.all_gather(first_part, 'dp', axis=0, tiled=True)  134 us
    reduce_scatter x1, waiting for transfers between devices, per_device(): lax.psum_scatter(outer_sum(mixed_piece, active_cols).astype(jnp.bfloat16)...  72.3 us
    all_gather x1, waiting for transfers between devices, per_device(): lax.all_gather(second_part, 'dp', axis=0, tiled=True)  70.6 us
    reduce_scatter x1, waiting for transfers between devices, per_device(): lax.psum_scatter(outer_sum(two_piece, inner_cols).astype(jnp.bfloat16), '...  69.4 us
    all_gather x1, waiting for transfers between devices, per_device(): lax.all_gather(key_part, 'dp', axis=0, tiled=True)  48.6 us
    all_gather x1, waiting for transfers between devices, per_device(): lax.all_gather(query_part, 'dp', axis=0, tiled=True)  48 us
    all_to_all x1, waiting for transfers between devices, per_device(): lax.all_to_all(stacked, 'seq', split_axis=3, concat_axis=2, tiled=True)  40.9 us
    all_to_all x1, waiting for transfers between devices, per_device(): lax.all_to_all(grad_stacked, 'seq', split_axis=2, concat_axis=3, tiled=True)  40.5 us
  transfers between devices with their start and end apart: 27, of which 15 were waited for; matrix products, arithmetic and copies ran while one was open for 26% of the time, Pallas kernels for 0%

commit v1 on v0

v1 whole, which is shorter than its diff:
```python
import jax
import jax.numpy as jnp
from jax import lax
from jax.sharding import PartitionSpec as P

HEAD_DIM = 72
SLOTS = 736
VALID = 729


EPSILON = 1e-06
NEGATIVE = -1000000000.0


def layer_norm(values, gain, shift):
    centred = values - jnp.mean(values, axis=-1, keepdims=True)
    spread = jnp.mean(centred * centred, axis=-1, keepdims=True)
    return centred * lax.rsqrt(spread + EPSILON) * gain + shift


def gelu_tanh(values):
    return jax.nn.gelu(values, approximate=True)


def times_weight(left_side, right_side):
    return jnp.dot(left_side, right_side, preferred_element_type=jnp.float32)


def times_transposed(left_side, right_side):
    return lax.dot_general(
        left_side, right_side, (((1,), (1,)), ((), ())), preferred_element_type=jnp.float32
    )


def outer_sum(left_side, right_side):
    return lax.dot_general(
        left_side, right_side, (((0,), (0,)), ((), ())), preferred_element_type=jnp.float32
    )


def split_heads(stacked):
    slot_count = stacked.shape[1]
    local_heads = stacked.shape[2] // HEAD_DIM
    return (
        stacked[0].reshape(slot_count, local_heads, HEAD_DIM),
        stacked[1].reshape(slot_count, local_heads, HEAD_DIM),
        stacked[2].reshape(slot_count, local_heads, HEAD_DIM),
    )


def head_scores(query_heads, key_heads, slot_live):
    scores = jnp.einsum(
        "qhd,khd->hqk", query_heads, key_heads, preferred_element_type=jnp.float32
    ) * HEAD_DIM ** (-0.5)
    return jnp.where(slot_live[None, None, :], scores, NEGATIVE)


def attend_image(stacked, slot_live):
    query_heads, key_heads, value_heads = split_heads(stacked)
    scores = head_scores(query_heads, key_heads, slot_live)
    highest = jnp.max(scores, axis=-1, keepdims=True)
    raised = jnp.exp(scores - highest)
    total = jnp.sum(raised, axis=-1, keepdims=True)
    probs = (raised / total).astype(jnp.bfloat16)
    context = jnp.einsum("hqk,khd->qhd", probs, value_heads, preferred_element_type=jnp.float32)
    context = context.reshape(stacked.shape[1], stacked.shape[2]).astype(jnp.bfloat16)
    return (context, (highest + jnp.log(total))[..., 0])


def attend_back(stacked, log_total, grad_context, slot_live):
    query_heads, key_heads, value_heads = split_heads(stacked)
    grad_heads = grad_context.reshape(query_heads.shape)
    scores = head_scores(query_heads, key_heads, slot_live)
    probs = jnp.exp(scores - log_total[..., None])
    grad_probs = jnp.einsum(
        "qhd,khd->hqk", grad_heads, value_heads, preferred_element_type=jnp.float32
    )
    row_inner = jnp.sum(probs * grad_probs, axis=-1, keepdims=True)
    grad_scores = (probs * (grad_probs - row_inner)).astype(jnp.bfloat16)
    scale = HEAD_DIM ** (-0.5)
    grad_query = (
        jnp.einsum("hqk,khd->qhd", grad_scores, key_heads, preferred_element_type=jnp.float32)
        * scale
    )
    grad_key = (
        jnp.einsum("hqk,qhd->khd", grad_scores, query_heads, preferred_element_type=jnp.float32)
        * scale
    )
    grad_value = jnp.einsum(
        "hqk,qhd->khd", probs.astype(jnp.bfloat16), grad_heads, preferred_element_type=jnp.float32
    )
    shape_out = (stacked.shape[1], stacked.shape[2])
    return jnp.stack(
        [
            grad_query.reshape(shape_out).astype(jnp.bfloat16),
            grad_key.reshape(shape_out).astype(jnp.bfloat16),
            grad_value.reshape(shape_out).astype(jnp.bfloat16),
        ],
        axis=0,
    )


def per_device(
    embeds,
    image_counts,
    norm1_gain,
    norm1_bias,
    query_weight,
    query_bias,
    key_weight,
    value_weight,
    value_bias,
    out_weight,
    out_bias,
    norm2_gain,
    norm2_bias,
    fc1_weight,
    fc1_bias,
    fc2_weight,
    fc2_bias,
    out_grad,
):
    images, rows_dev, width = embeds.shape
    token_count = images * rows_dev
    columns = query_weight.shape[1]
    hidden = fc1_weight.shape[1]
    position = lax.axis_index("seq") * rows_dev + jnp.arange(rows_dev, dtype=jnp.int32)
    slot_live = jnp.arange(SLOTS, dtype=jnp.int32) < VALID
    image_live = jnp.arange(images, dtype=jnp.int32) < image_counts[0]
    row_mask = (
        jnp.where(image_live[:, None] & (position < VALID)[None, :], 1.0, 0.0)
        .astype(jnp.float32)
        .reshape(token_count)
    )
    low = jnp.bfloat16
    attention_low = jnp.concatenate([query_weight, key_weight, value_weight], axis=1).astype(low)
    attention_full = lax.all_gather(attention_low, "dp", axis=0, tiled=True)
    rest_low = jnp.concatenate([out_weight, fc1_weight, fc2_weight], axis=1).astype(low)
    rest_full = lax.all_gather(rest_low, "dp", axis=0, tiled=True)
    out_part = rest_full[:, :columns]
    first_part = rest_full[:, columns : columns + hidden]
    second_part = rest_full[:, columns + hidden :]
    packed = jnp.stack(
        [norm1_gain, norm1_bias, out_bias, norm2_gain, norm2_bias, fc2_bias], axis=0
    ).astype(low)
    vectors = lax.all_gather(packed, "seq", axis=1, tiled=True).astype(jnp.float32)
    gain_one, bias_one, attend_shift, gain_two, bias_two, second_shift = [vectors[i] for i in range(6)]
    query_shift = query_bias.astype(low).astype(jnp.float32)
    value_shift = value_bias.astype(low).astype(jnp.float32)
    first_shift = fc1_bias.astype(low).astype(jnp.float32)

    embed_rows = embeds.reshape(token_count, width).astype(jnp.float32)
    normed_one = layer_norm(embed_rows, gain_one, bias_one).astype(low)
    one_all = lax.all_gather(
        normed_one.reshape(images, rows_dev, width), "seq", axis=1, tiled=True
    ).reshape(images * SLOTS, width)
    grad_mixed = out_grad.reshape(token_count, width).astype(jnp.float32) * row_mask[:, None]
    grad_mixed_low = grad_mixed.astype(low)
    mixed_all = lax.all_gather(
        grad_mixed_low.reshape(images, rows_dev, width), "seq", axis=1, tiled=True
    ).reshape(images * SLOTS, width)

    shift_all = jnp.concatenate([query_shift, jnp.zeros_like(query_shift), value_shift])
    heads_all = (times_weight(one_all, attention_full) + shift_all).astype(low)
    by_heads = heads_all.reshape(images, SLOTS, 3, columns).transpose(0, 2, 1, 3)
    context_heads, log_total = lax.map(lambda element: attend_image(element, slot_live), by_heads)
    context = lax.all_to_all(context_heads, "seq", split_axis=1, concat_axis=2, tiled=True).reshape(
        token_count, width
    )
    out_full = lax.all_gather(out_part, "seq", axis=1, tiled=True)
    residual = embed_rows + times_weight(context, out_full) + attend_shift
    normed_two = layer_norm(residual, gain_two, bias_two).astype(low)
    two_all = lax.all_gather(
        normed_two.reshape(images, rows_dev, width), "seq", axis=1, tiled=True
    ).reshape(images * SLOTS, width)
    inner = times_weight(two_all, first_part) + first_shift
    activated = gelu_tanh(inner).astype(low)
    grad_active = times_weight(mixed_all, second_part)
    grad_inner = jax.vjp(gelu_tanh, inner)[1](grad_active)[0].astype(low)

    def scatter_rows(partial):
        parts = partial.astype(low).reshape(images, SLOTS, width)
        arrived = lax.all_to_all(
            parts.reshape(images, -1, rows_dev, width), "seq", split_axis=1, concat_axis=1, tiled=True
        )
        return jnp.sum(arrived.astype(jnp.float32), axis=1).reshape(token_count, width)

    grad_normed_two = scatter_rows(times_transposed(grad_inner, first_part))
    mixed = scatter_rows(times_transposed(activated, second_part)) + second_shift
    output = (
        ((residual + mixed) * row_mask[:, None]).astype(low).reshape(images, rows_dev, width)
    )
    second_shift_grad = jnp.sum(grad_mixed, axis=0)
    norm_two_pull = jax.vjp(layer_norm, residual, gain_two, bias_two)[1]
    grad_norm_input, gain_two_grad, bias_two_grad = norm_two_pull(grad_normed_two)
    grad_residual = grad_mixed + grad_norm_input
    grad_attended = grad_residual.astype(low)
    attended_all = lax.all_gather(
        grad_attended.reshape(images, rows_dev, width), "seq", axis=1, tiled=True
    ).reshape(images * SLOTS, width)
    out_rows = lax.dynamic_slice_in_dim(
        out_full, lax.axis_index("seq") * columns, columns, axis=0
    )
    grad_context = times_transposed(attended_all, out_rows).astype(low)
    fc_grads = jnp.concatenate(
        [outer_sum(two_all, grad_inner).astype(low), outer_sum(mixed_all, activated).astype(low)], axis=1
    )
    fc_owned = lax.psum_scatter(fc_grads, "dp", scatter_dimension=0, tiled=True).astype(jnp.float32)
    out_grad_rows = outer_sum(context_heads.reshape(images * SLOTS, columns), attended_all).astype(low)
    out_grad_cols = lax.all_to_all(out_grad_rows, "seq", split_axis=1, concat_axis=0, tiled=True)
    grad_stacked = lax.map(
        lambda element: attend_back(element[0], element[1], element[2], slot_live),
        (by_heads, log_total, grad_context.reshape(images, SLOTS, columns)),
    )
    grad_heads_all = grad_stacked.transpose(0, 2, 1, 3).reshape(images * SLOTS, 3 * columns)
    attention_grads = jnp.concatenate(
        [outer_sum(one_all, grad_heads_all).astype(low), out_grad_cols], axis=1
    )
    attention_owned = lax.psum_scatter(
        attention_grads, "dp", scatter_dimension=0, tiled=True
    ).astype(jnp.float32)
    grad_normed_one = scatter_rows(times_transposed(grad_heads_all, attention_full))
    norm_one_pull = jax.vjp(layer_norm, embed_rows, gain_one, bias_one)[1]
    grad_embed_norm, gain_one_grad, bias_one_grad = norm_one_pull(grad_normed_one)
    embeds_grad = (grad_residual + grad_embed_norm).astype(low).reshape(images, rows_dev, width)
    whole = jnp.stack(
        [
            gain_one_grad,
            bias_one_grad,
            jnp.sum(grad_attended.astype(jnp.float32), axis=0),
            gain_two_grad,
            bias_two_grad,
            second_shift_grad,
        ],
        axis=0,
    )
    owned = lax.psum_scatter(whole, "seq", scatter_dimension=1, tiled=True)
    head_sums = jnp.sum(grad_heads_all.astype(jnp.float32), axis=0)
    query_shift_grad = head_sums[:columns]
    value_shift_grad = head_sums[2 * columns :]
    first_shift_grad = jnp.sum(grad_inner.astype(jnp.float32), axis=0)
    owned, query_shift_grad, value_shift_grad, first_shift_grad = lax.psum(
        (owned, query_shift_grad, value_shift_grad, first_shift_grad), "dp"
    )
    return (
        output,
        embeds_grad,
        owned[0],
        owned[1],
        attention_owned[:, :columns],
        query_shift_grad,
        attention_owned[:, columns : 2 * columns],
        attention_owned[:, 2 * columns : 3 * columns],
        value_shift_grad,
        attention_owned[:, 3 * columns :],
        owned[2],
        owned[3],
        owned[4],
        fc_owned[:, :hidden],
        first_shift_grad,
        fc_owned[:, hidden:],
        owned[5],
    )


def solution(mesh):
    in_specs = (
        P("dp", "seq", None),
        P("dp"),
        P("seq"),
        P("seq"),
        P("dp", "seq"),
        P("seq"),
        P("dp", "seq"),
        P("dp", "seq"),
        P("seq"),
        P("dp", "seq"),
        P("seq"),
        P("seq"),
        P("seq"),
        P("dp", "seq"),
        P("seq"),
        P("dp", "seq"),
        P("seq"),
        P("dp", "seq", None),
    )
    out_specs = (
        P("dp", "seq", None),
        P("dp", "seq", None),
        P("seq"),
        P("seq"),
        P("dp", "seq"),
        P("seq"),
        P("dp", "seq"),
        P("dp", "seq"),
        P("seq"),
        P("dp", "seq"),
        P("seq"),
        P("seq"),
        P("seq"),
        P("dp", "seq"),
        P("seq"),
        P("dp", "seq"),
        P("seq"),
    )
    return jax.shard_map(
        per_device, mesh=mesh, in_specs=in_specs, out_specs=out_specs, check_vma=False
    )
```

time: 1190 us -> 684 us (0.57)
  waiting for transfers between devices: 654 us -> 317 us
  local copies, waits for them, and re-layouts: 166 us -> 81.1 us
  blocking collectives: 113 us -> 63 us
  starting transfers between devices: 39.1 us -> 20.5 us
  matrix products: 134 us -> 122 us
    all_gather x12 -> x7, waiting for transfers between devices: 338 us -> 193 us  [the longest x1 79.3 us: per_device(): rest_full = lax.all_gather(rest_low, 'dp', axis=0, tiled=True)]
    reduce_scatter x6 -> x0, waiting for transfers between devices: 142 us -> none  [the longest x1 72.3 us: per_device(): lax.psum_scatter(outer_sum(mixed_piece, active_cols).astype(jnp.bfloat16)...]
    all_to_all x26 -> x3, local copies, waits for them, and re-layouts: 94.5 us -> 3.49 us  [per_device(): lax.all_to_all(out_grad_rows, 'seq', split_axis=1, concat_axis=0, tiled=T...]
    all_to_all x9 -> x4, waiting for transfers between devices: 173 us -> 91 us  [the longest x3 91 us: scatter_rows(): lax.all_to_all(parts.reshape(images, -1, rows_dev, width), 'seq', split_a...]
    unnamed x18 -> x13, waiting for transfers between devices: 1.32 us -> 33.1 us
    all_gather x4 -> x1, blocking collectives: 33.2 us -> 6.27 us  [per_device(): lax.all_gather(packed, 'seq', axis=1, tiled=True).astype(jnp.float32)]
    unnamed x2 -> x0, blocking collectives: 23 us -> none
    while x17 -> x4, local copies, waits for them, and re-layouts: 18.6 us -> 0.01 us  [the longest x1 12 us: per_device(): lax.map(lambda element: attend_back(element[0], element[1], element[2], s...]
  transfers between devices with their start and end apart: 27 -> 14, of which waited for: 15 -> 10; matrix products, arithmetic and copies ran while one was open for 26% -> 30% of each run, Pallas kernels for 0% -> 0%
where the time goes in v1:
time: 684 us; the launch traced here: 676 us
  waiting for transfers between devices  317 us (46%)
  matrix products  122 us (18%)
  local copies, waits for them, and re-layouts  81.1 us (12%)
  blocking collectives  63 us (9%)
  other arithmetic  56.4 us (8%)
  starting transfers between devices  20.5 us (3%)
  between operations  15.8 us (2%)
    all_to_all x3, waiting for transfers between devices, scatter_rows(): lax.all_to_all(parts.reshape(images, -1, rows_dev, width), 'seq', split_a...  91 us
    all_gather x1, waiting for transfers between devices, per_device(): rest_full = lax.all_gather(rest_low, 'dp', axis=0, tiled=True)  79.3 us
    psum x1, blocking collectives, per_device(): lax.psum((owned, query_shift_grad, value_shift_grad, first_shift_grad), '...  37.9 us
    dot_general x4, matrix products, times_weight(): return jnp.dot(left_side, right_side, preferred_element_type=jnp.float32)  36.5 us
    all_gather x1, waiting for transfers between devices, per_device(): attention_full = lax.all_gather(attention_low, 'dp', axis=0, tiled=True)  34.9 us
    unnamed x13, waiting for transfers between devices  33.1 us
    unnamed x92, local copies, waits for them, and re-layouts  33 us
    dot_general x4, matrix products, times_transposed(): lax.dot_general(left_side, right_side, (((1,), (1,)), ((), ())), preferre...  31.5 us
  transfers between devices with their start and end apart: 14, of which 10 were waited for; matrix products, arithmetic and copies ran while one was open for 30% of the time, Pallas kernels for 0%

profile of v1, /device:TPU:0, one launch (start us, length us, event | category | flops | bytes accessed | tf_op | source)
XLA Modules:
  0.0 675.9 jit_solution(3234601499509209351)
XLA Ops:
  15.5 6.3 all-gather
  27.9 34.9 %all-gather.11.cloned.1.call-done = bf16[1152,864]{1,0:T(8,128)(2,1)} async-done(((bf16[144,864]{1,0:T(8,128)(2,1)}), bf16[1152,864]{1,0:T(8,128)(2,1)}) %all-gather.11.cloned.1.call-update) | async-done | bytes 1990672 | tf_op jit(solution)/shard_map/all_gather | solution.py:137
  62.9 30.7 %all-gather.9.cloned.1.call-done = bf16[2,736,1152]{2,1,0:T(8,128)(2,1)} async-done(((bf16[2,184,1152]{2,1,0:T(8,128)(2,1)}), bf16[2,736,1152]{2,1,0:T(8,128)(2,1)}) %all-gather.9.cloned.1.call-update) | async-done | bytes 3391504 | tf_op jit(solution)/shard_map/all_gather | solution.py:154
  93.5 8.1 %add_convert_fusion = bf16[1472,864]{1,0:T(8,128)(2,1)} fusion(bf16[1472,1152]{1,0:T(8,128)(2,1)} %bitcast.217, bf16[1152,864]{1,0:T(8,128)(2,1)} %all-gather.11.cloned.1.call-done, f32[864]{0:T(1024)S(1)} %pad_maximum_fusion.3), kind=kOutput, calls=%fused_computation.61 | convolution fusion | flops 2932789248 | bytes 7929216 | tf_op jit(solution)/shard_map/dot_general | solution.py:26
  110.9 79.3 %all-gather.13.cloned.1.call-done = bf16[1152,2440]{1,0:T(8,128)(2,1)} async-done(((bf16[144,2440]{1,0:T(8,128)(2,1)}), bf16[1152,2440]{1,0:T(8,128)(2,1)}) %all-gather.13.cloned.1.call-update) | async-done | bytes 5621776 | tf_op jit(solution)/shard_map/all_gather | solution.py:139
  195.2 15.5 %while.24 = (s32[]{:T(128)}, bf16[2,736,288]{1,2,0:T(8,128)(2,1)}, f32[2,4,736]{2,1,0:T(4,128)S(1)}, bf16[2,3,736,288]{2,3,1,0:T(8,128)(2,1)S(1)}, s32[]{:T(128)}, /*index=5*/s32[]{:T(128)}, s32[]{}, s32[]{}) while((s32[]{:T(128)}, bf16[2,736,288]{1,2,0:T(8,128)(2,1)}, f32[2,4,736]{2,1,0:T(4,128)S(1)}, ...), condition=%wide.region_5.6_spmd.clone, body=%wide.region_2.5_spmd.clone.sunk | while | flops 650244992 | bytes 31206396 | solution.py:166
  210.7 4.7 copy.117
  215.4 18.8 %all_to_all.49 = bf16[2,736,288]{2,0,1:T(2,128)(2,1)S(1)} all-to-all(bf16[2,736,288]{2,0,1:T(2,128)(2,1)} %copy.117), channel_id=1, replica_groups=mesh['dp'=8,'seq'=4] {'seq'}, dimensions={1} | all-to-all | bytes 1695744 | tf_op jit(solution)/shard_map/all_to_all | solution.py:167
  247.2 24.6 %all-gather.17.cloned.1.call-done = bf16[2,736,1152]{2,1,0:T(8,128)(2,1)} async-done(((bf16[2,184,1152]{2,1,0:T(8,128)(2,1)}), bf16[2,736,1152]{2,1,0:T(8,128)(2,1)}) %all-gather.17.cloned.1.call-update) | async-done | bytes 3391504 | tf_op jit(solution)/shard_map/all_gather | solution.py:173
  271.8 10.8 %convolution_add_fusion = f32[1472,1076]{0,1:T(8,128)} fusion(bf16[1472,1152]{1,0:T(8,128)(2,1)} %bitcast.219, f32[1076]{0:T(1024)S(1)} %convert_convert_fusion, bf16[1152,2440]{1,0:T(8,128)(2,1)} %all-gather.13.cloned.1.call-done), kind=kOutput, calls=%fused_computation.40 | convolution fusion | flops 3650824960 | bytes 12385488 | tf_op jit(solution)/shard_map/dot_general | solution.py:26
  282.6 21.1 %all-gather.19.cloned.1.call-done = bf16[2,736,1152]{2,1,0:T(8,128)(2,1)} async-done(((bf16[2,184,1152]{2,1,0:T(8,128)(2,1)}), bf16[2,736,1152]{2,1,0:T(8,128)(2,1)}) %all-gather.19.cloned.1.call-update) | async-done | bytes 3391504 | tf_op jit(solution)/shard_map/all_gather | solution.py:159
  303.7 14.1 %convert_reduce_fusion.5 = (f32[1076]{0:T(1024)}, bf16[1472,1076]{0,1:T(8,128)(2,1)S(1)}) fusion(f32[1472,1076]{0,1:T(8,128)} %convolution_add_fusion, bf16[1472,1152]{1,0:T(8,128)(2,1)} %bitcast.221, bf16[1152,2440]{1,0:T(8,128)(2,1)} %all-gather.13.cloned.1.call-done), kind=kOutput, calls=%fused_computation.58 | convolution fusion | flops 3684085248 | bytes 15853264 | tf_op jit(solution)/shard_map/dot_general | solution.py:26
  317.8 10.1 %convolution_convert_fusion.3 = bf16[1472,1152]{1,0:T(8,128)(2,1)S(1)} fusion(bf16[1472,1076]{0,1:T(8,128)(2,1)S(1)} %get-tuple-element.302, bf16[1152,2440]{1,0:T(8,128)(2,1)} %all-gather.13.cloned.1.call-done), kind=kOutput, calls=%fused_computation.48 | convolution fusion | flops 3650936832 | bytes 9213440 | tf_op jit(solution)/shard_map/dot_general | solution.py:30
  329.9 5.1 all-to-all-start.2
  335.0 10.7 %convolution_convert_fusion.4 = bf16[1472,1152]{1,0:T(8,128)(2,1)S(1)} fusion(bf16[1152,2440]{1,0:T(8,128)(2,1)} %all-gather.13.cloned.1.call-done, f32[1472,1076]{0,1:T(8,128)} %convolution_add_fusion), kind=kOutput, calls=%fused_computation.49 | convolution fusion | flops 3665191680 | bytes 12681216 | tf_op jit(solution)/shard_map/dot_general | solution.py:30
  347.8 26.8 %all-to-all-done.2 = bf16[2,4,184,1152]{3,2,0,1:T(8,128)(2,1)} async-done(((bf16[2,4,184,1152]{3,2,0,1:T(8,128)(2,1)}), bf16[2,4,184,1152]{3,2,0,1:T(8,128)(2,1)}, u32[]{:S(2)}, u32[]{:S(2)}) %all-to-all-start.2) | async-done | bytes 3391520 | tf_op jit(solution)/shard_map/all_to_all | solution.py:183
  374.6 4.7 all-to-all-start.1
  385.0 33.9 %all-to-all-done.1 = bf16[2,4,184,1152]{3,2,0,1:T(8,128)(2,1)} async-done(((bf16[2,4,184,1152]{3,2,0,1:T(8,128)(2,1)}), bf16[2,4,184,1152]{3,2,0,1:T(8,128)(2,1)}, u32[]{:S(2)}, u32[]{:S(2)}) %all-to-all-start.1) | async-done | bytes 3391520 | tf_op jit(solution)/shard_map/all_to_all | solution.py:183
  426.8 7.6 %convolution_convert_fusion.1 = bf16[1152,1076]{0,1:T(8,128)(2,1)S(1)} fusion(bf16[1472,1152]{1,0:T(8,128)(2,1)} %bitcast.220, bf16[1472,1076]{0,1:T(8,128)(2,1)} %copy-done.39), kind=kOutput, calls=%fused_computation.46 | convolution fusion | flops 3650480640 | bytes 9038336 | tf_op jit(solution)/shard_map/dot_general | solution.py:36
  434.4 8.6 %convolution_convert_fusion = bf16[1152,1076]{0,1:T(8,128)(2,1)S(1)} fusion(bf16[1472,1152]{1,0:T(8,128)(2,1)S(1)} %bitcast.222, f32[1472,1076]{0,1:T(8,128)} %convolution_add_fusion), kind=kOutput, calls=%fused_computation.45 | convolution fusion | flops 3664735488 | bytes 12206080 | tf_op jit(solution)/shard_map/dot_general | solution.py:36
  445.9 8.4 %copy.146 = bf16[1152,2152]{1,0:T(8,128)(2,1)} copy(bf16[1152,2152]{0,1:T(8,128)(2,1)} %pad_maximum_fusion) | data formatting | bytes 9916416
  461.5 4.4 all-to-all-start.4
  465.9 4.2 convolution_convert_fusion.6
  473.2 26.9 %while.25 = (s32[]{:T(128)}, bf16[2,3,736,288]{2,3,1,0:T(8,128)(2,1)}, bf16[2,3,736,288]{2,3,1,0:T(8,128)(2,1)S(1)}, f32[2,4,736]{2,1,0:T(4,128)}, bf16[2,736,28...) while((s32[]{:T(128)}, bf16[2,3,736,288]{2,3,1,0:T(8,128)(2,1)}, ...), condition=%wide.region_14.15_spmd.clone, body=%wide.region_12.14_spmd.clone.sunk | while | flops 1597459328 | bytes 75413536 | solution.py:211
  500.1 4.5 copy.125
  508.0 6.5 convolution_convert_fusion.2
  516.5 5.0 all-to-all-start.3
  521.7 6.9 %convolution_convert_fusion.5 = bf16[1152,864]{0,1:T(8,128)(2,1)} fusion(bf16[1472,864]{0,1:T(8,128)(2,1)S(1)} %copy-done.10, bf16[1472,1152]{1,0:T(8,128)(2,1)} %bitcast.218), kind=kOutput, calls=%fused_computation.63 | convolution fusion | flops 2931240960 | bytes 7925760 | tf_op jit(solution)/shard_map/dot_general | solution.py:36
  530.8 30.3 %all-to-all-done.3 = bf16[2,4,184,1152]{3,2,0,1:T(8,128)(2,1)} async-done(((bf16[2,4,184,1152]{3,2,0,1:T(8,128)(2,1)}), bf16[2,4,184,1152]{3,2,0,1:T(8,128)(2,1)}, u32[]{:S(2)}, u32[]{:S(2)}) %all-to-all-start.3) | async-done | bytes 3391520 | tf_op jit(solution)/shard_map/all_to_all | solution.py:183
  570.5 5.3 copy.144
  592.9 37.9 %all-reduce = (f32[6,288]{1,0:T(8,128)S(1)}, f32[288]{0:T(512)}, f32[288]{0:T(512)}, f32[1076]{0:T(1024)}) all-reduce(f32[6,288]{1,0:T(8,128)S(1)} %copy.143, f32[288]{0:T(512)S(1)} %get-tuple-element.249, f32[288]{0:T(512)S(1)} %get-tuple-element.248, f32[1076]{0:T(1024)S(1)} %copy-done.33), channel_id=1, replica_groups=mesh['dp'=8,'seq'=4] {'dp'}, use_global_device_ids=true, to_apply=%region_25.26 | all-reduce | flops 3380 | bytes 27040 | tf_op jit(solution)/shard_map/psum | solution.py:242
  631.4 32.9 %reduce-scatter.12.cloned.1.call-done = bf16[144,1152]{1,0:T(8,128)(2,1)} async-done(((bf16[1152,1152]{1,0:T(8,128)(2,1)}), bf16[144,1152]{1,0:T(8,128)(2,1)}) %reduce-scatter.12.cloned.1.call-update) | async-done | bytes 331792
  (249 shorter events, 152.4 us)
Async XLA Ops:
  7.2 16.6 %copy-start = (bf16[2,184,1152]{2,1,0:T(8,128)(2,1)S(1)}, bf16[2,184,1152]{2,1,0:T(8,128)(2,1)}, u32[]{:S(2)}) copy-start(bf16[2,184,1152]{2,1,0:T(8,128)(2,1)} %param.22) | copy-start | bytes 2543620
  7.2 19.0 %copy-start.11 = (f32[144,1076]{1,0:T(8,128)S(1)}, f32[144,1076]{1,0:T(8,128)}, u32[]{:S(2)}) copy-start(f32[144,1076]{1,0:T(8,128)} %param.35) | copy-start | bytes 1859332
  7.2 55.7 %all-gather.11.cloned.1.call-start = ((), (), s32[]{:S(2)}) async-start(), calls=%async_computation.9 | async-start | bytes 2322432 | tf_op jit(solution)/shard_map/all_gather | solution.py:137
  9.3 17.0 %copy-start.12 = (f32[144,1076]{1,0:T(8,128)S(1)}, f32[144,1076]{1,0:T(8,128)}, u32[]{:S(2)}) copy-start(f32[144,1076]{1,0:T(8,128)} %param.37) | copy-start | bytes 1859332
  11.2 15.1 %copy-start.13 = (f32[144,288]{1,0:T(8,128)S(1)}, f32[144,288]{1,0:T(8,128)}, u32[]{:S(2)}) copy-start(f32[144,288]{1,0:T(8,128)} %param.31) | copy-start | bytes 497668
  11.2 82.3 %all-gather.9.cloned.1.call-start = ((), (), s32[]{:S(2)}) async-start(), calls=%async_computation.8 | async-start | bytes 4239360 | tf_op jit(solution)/shard_map/all_gather | solution.py:154
  26.1 164.1 %all-gather.13.cloned.1.call-start = ((), (), s32[]{:S(2)}) async-start(), calls=%async_computation.10 | async-start | bytes 6635520 | tf_op jit(solution)/shard_map/all_gather | solution.py:139
  27.7 210.7 %all-gather.15.cloned.1.call-start = ((), (), s32[]{:S(2)}) async-start(), calls=%async_computation.11 | async-start | bytes 3317760 | tf_op jit(solution)/shard_map/all_gather | solution.py:170
  194.7 77.1 %all-gather.17.cloned.1.call-start = ((), (), s32[]{:S(2)}) async-start(), calls=%async_computation.12 | async-start | bytes 4239360 | tf_op jit(solution)/shard_map/all_gather | solution.py:173
  210.7 27.7 %copy-start.16 = (f32[2,4,736]{2,1,0:T(4,128)}, f32[2,4,736]{2,1,0:T(4,128)S(1)}, u32[]{:S(2)}) copy-start(f32[2,4,736]{2,1,0:T(4,128)S(1)} %get-tuple-element.408) | copy-start | bytes 70660
  244.4 59.3 %all-gather.19.cloned.1.call-start = ((), (), s32[]{:S(2)}) async-start(), calls=%async_computation.13 | async-start | bytes 4239360 | tf_op jit(solution)/shard_map/all_gather | solution.py:159
  317.8 10.1 %copy-start.39 = (bf16[1472,1076]{0,1:T(8,128)(2,1)}, bf16[1472,1076]{0,1:T(8,128)(2,1)S(1)}, u32[]{:S(2)}) copy-start(bf16[1472,1076]{0,1:T(8,128)(2,1)S(1)} %get-tuple-element.302) | copy-start | bytes 9503236
  329.9 44.7 %all-to-all-start.2 = ((bf16[2,4,184,1152]{3,2,0,1:T(8,128)(2,1)}), bf16[2,4,184,1152]{3,2,0,1:T(8,128)(2,1)}, u32[]{:S(2)}, u32[]{:S(2)}) async-start(bf16[2,4,184,1152]{3,2,0,1:T(8,128)(2,1)} %copy.122), calls=%async_computation.2 | async-start | bytes 6782976 | tf_op jit(solution)/shard_map/all_to_all | solution.py:183
  374.6 44.3 %all-to-all-start.1 = ((bf16[2,4,184,1152]{3,2,0,1:T(8,128)(2,1)}), bf16[2,4,184,1152]{3,2,0,1:T(8,128)(2,1)}, u32[]{:S(2)}, u32[]{:S(2)}) async-start(bf16[2,4,184,1152]{3,2,0,1:T(8,128)(2,1)} %copy.121), calls=%async_computation.1 | async-start | bytes 6782976 | tf_op jit(solution)/shard_map/all_to_all | solution.py:183
  379.3 77.3 %all-gather.21.cloned.1.call-start = ((), (), s32[]{:S(2)}) async-start(), calls=%async_computation.14 | async-start | bytes 4239360 | tf_op jit(solution)/shard_map/all_gather | solution.py:198
  379.4 44.0 %copy-start.25 = (f32[368]{0:T(512)}, f32[368]{0:T(512)S(1)}, u32[]{:S(2)}) copy-start(f32[368]{0:T(512)S(1)} %select_n.23) | copy-start | bytes 4420
  385.0 36.8 %copy-start.20 = (f32[1152]{0:T(1024)S(1)}, f32[1152]{0:T(1024)}, u32[]{:S(2)}) copy-start(f32[1152]{0:T(1024)} %get-tuple-element.236) | copy-start | bytes 13828
  423.4 10.9 %copy-start.31 = (f32[368]{0:T(512)}, f32[368]{0:T(512)S(1)}, u32[]{:S(2)}) copy-start(f32[368]{0:T(512)S(1)} %negate_multiply_fusion.1) | copy-start | bytes 4420
  426.5 151.7 %reduce-scatter.14.cloned.1.call-start = ((), (), s32[]{:S(2)}) async-start(), calls=%async_computation.17 | async-start | bytes 5640192
  426.8 7.6 %copy-start.38 = (bf16[2,736,1152]{2,1,0:T(8,128)(2,1)S(1)}, bf16[2,736,1152]{2,1,0:T(8,128)(2,1)}, u32[]{:S(2)}) copy-start(bf16[2,736,1152]{2,1,0:T(8,128)(2,1)} %all-gather.19.cloned.1.call-done) | copy-start | bytes 10174468
  461.5 55.0 %all-to-all-start.4 = ((bf16[288,4,288]{0,2,1:T(8,128)(2,1)}), bf16[288,4,288]{0,2,1:T(8,128)(2,1)}, u32[]{:S(2)}, u32[]{:S(2)}) async-start(bf16[288,4,288]{0,2,1:T(8,128)(2,1)} %bitcast.26), calls=%async_computation.4 | async-start | bytes 1769472 | tf_op jit(solution)/shard_map/all_to_all | solution.py:210
  516.5 44.6 %all-to-all-start.3 = ((bf16[2,4,184,1152]{3,2,0,1:T(8,128)(2,1)}), bf16[2,4,184,1152]{3,2,0,1:T(8,128)(2,1)}, u32[]{:S(2)}, u32[]{:S(2)}) async-start(bf16[2,4,184,1152]{3,2,0,1:T(8,128)(2,1)} %copy.126), calls=%async_computation.3 | async-start | bytes 6782976 | tf_op jit(solution)/shard_map/all_to_all | solution.py:183
  521.5 70.4 %reduce-scatter.10.cloned.1.call-start = ((), (), s32[]{:S(2)}) async-start(), calls=%async_computation.15 | async-start | bytes 737280
  530.1 34.5 %copy-start.1 = (bf16[2,184,1152]{2,1,0:T(8,128)(2,1)S(1)}, bf16[2,184,1152]{2,1,0:T(8,128)(2,1)}, u32[]{:S(2)}) copy-start(bf16[2,184,1152]{2,1,0:T(8,128)(2,1)} %param.22) | copy-start | bytes 2543620
  530.2 34.5 %copy-start.15 = (f32[1152]{0:T(1024)S(1)}, f32[1152]{0:T(1024)}, u32[]{:S(2)}) copy-start(f32[1152]{0:T(1024)} %copy-done.14) | copy-start | bytes 13828
  530.2 34.5 %copy-start.19 = (f32[2,184]{1,0:T(2,128)S(1)}, f32[2,184]{1,0:T(2,128)}, u32[]{:S(2)}) copy-start(f32[2,184]{1,0:T(2,128)} %copy-done.18) | copy-start | bytes 4420
  530.7 34.4 %copy-start.30 = (f32[2,184]{1,0:T(2,128)S(1)}, f32[2,184]{1,0:T(2,128)}, u32[]{:S(2)}) copy-start(f32[2,184]{1,0:T(2,128)} %copy-done.29) | copy-start | bytes 4420
  530.8 34.4 %copy-start.28 = (f32[2,184]{1,0:T(2,128)S(1)}, f32[2,184]{1,0:T(2,128)}, u32[]{:S(2)}) copy-start(f32[2,184]{1,0:T(2,128)} %copy-done.27) | copy-start | bytes 4420
  567.2 97.1 %reduce-scatter.12.cloned.1.call-start = ((), (), s32[]{:S(2)}) async-start(), calls=%async_computation.16 | async-start | bytes 2985984
  580.5 7.9 %copy-start.9 = (bf16[2,184,1152]{2,1,0:T(8,128)(2,1)S(1)}, bf16[2,184,1152]{2,1,0:T(8,128)(2,1)}, u32[]{:S(2)}) copy-start(bf16[2,184,1152]{2,1,0:T(8,128)(2,1)} %param.39) | copy-start | bytes 2543620
  580.5 7.9 %copy-start.26 = (f32[368]{0:T(512)S(1)}, f32[368]{0:T(512)}, u32[]{:S(2)}) copy-start(f32[368]{0:T(512)} %copy-done.25) | copy-start | bytes 4420
  580.5 7.9 %copy-start.32 = (f32[368]{0:T(512)S(1)}, f32[368]{0:T(512)}, u32[]{:S(2)}) copy-start(f32[368]{0:T(512)} %copy-done.31) | copy-start | bytes 4420
  (23 other events, 80.6 us)
Sparse Core Ops, SparseCore 0:
  11.3 51.5 all-gather.10
  65.0 28.4 all-gather.8
  96.3 93.8 all-gather.12
  194.9 23.8 all-gather.14
  244.6 27.1 all-gather.16
  273.8 29.8 all-gather.18
  426.6 29.8 all-gather.20
  460.2 99.6 reduce-scatter.13
  567.3 22.0 reduce-scatter.9
  592.8 71.3 reduce-scatter.11
